TPU v7x, 32 devices: a whole 2x2x4 slice. The times are simulated.
32 devices in a mesh: row: 8 (over y, x, core), col: 4 (over z).
Axes of the slice: x: 2, y: 2, z: 4, core: 2. Of those that a mesh axis runs over, the one named last changes fastest.
Arguments:
- tokens: bfloat16 [65536, 1024], P('row', 'col'), may hold values from -6 to 6
- up_weight: bfloat16 [1024, 4096], P('row', 'col'), may hold values from -0.1875 to 0.1875
- hidden_grad: bfloat16 [65536, 4096], P('row', 'col'), may hold values from -6 to 6
Outputs:
- hidden: bfloat16 [65536, 4096], P('row', 'col')
- input_grad: bfloat16 [65536, 1024], P('row', 'col')
All inputs are finite; a program needn't handle non-finite values.
Results may differ from a plain program's by a relative error of at most 0.017.
Values may be sent and summed in bfloat16 or wider, within the bound.
No kernel may reach another device: no remote copies, remote signals or barrier semaphores. Data moves between devices by JAX's collectives and lax.ppermute only.
A program may use at most 128 MiB of HBM per device.

v0:
```python
import jax
import jax.numpy as jnp
from jax import lax
from jax.sharding import PartitionSpec as P

gelu_c = 0.7978845608028654
gelu_a = 0.044715


def gelu_value(v):
    inner = gelu_c * (v + gelu_a * v * v * v)
    return 0.5 * v * (1.0 + jnp.tanh(inner))


def gelu_slope(v):
    inner = gelu_c * (v + gelu_a * v * v * v)
    tval = jnp.tanh(inner)
    return 0.5 * (1.0 + tval) + 0.5 * v * (1.0 - tval * tval) * gelu_c * (
        1.0 + 3.0 * gelu_a * v * v
    )


def per_device(tokens, up_weight, hidden_grad):
    column_panel = lax.all_gather(up_weight, "row", axis=0, tiled=True)
    token_rows = lax.all_gather(tokens, "col", axis=1, tiled=True)
    preact = jnp.dot(token_rows, column_panel, preferred_element_type=jnp.float32)
    hidden = gelu_value(preact).astype(jnp.bfloat16)
    pre_grad = (hidden_grad.astype(jnp.float32) * gelu_slope(preact)).astype(jnp.bfloat16)
    summed = lax.psum_scatter(
        lax.dot_general(
            column_panel, pre_grad, (((1,), (1,)), ((), ())), preferred_element_type=jnp.float32
        ).astype(jnp.bfloat16),
        "col",
        scatter_dimension=0,
        tiled=True,
    ).astype(jnp.float32)
    input_grad = jnp.transpose(summed).astype(jnp.bfloat16)
    return (hidden, input_grad)


def solution(mesh):
    in_specs = (P("row", "col"), P("row", "col"), P("row", "col"))
    out_specs = (P("row", "col"), P("row", "col"))
    return jax.shard_map(
        per_device, mesh=mesh, in_specs=in_specs, out_specs=out_specs, check_vma=False
    )
```

profile of v0, /device:TPU:0, one launch (start us, length us, event | category | flops | bytes accessed | tf_op | source)
XLA Modules:
  0.0 688.1 jit_solution(10581565400900481184)
XLA Ops:
  7.2 0.0 all-gather.5.cloned.1.call-start
  7.2 0.7 all-gather.5.cloned.1.call-update
  7.9 0.0 all-gather.3.cloned.1.call-start
  7.9 0.7 all-gather.3.cloned.1.call-update
  8.6 0.0 reduce-scatter.2.cloned.1.call-start
  8.7 31.7 %all-gather.5.cloned.1.call-done = bf16[1024,1024]{1,0:T(8,128)(2,1)} async-done(((bf16[128,1024]{1,0:T(8,128)(2,1)}), bf16[1024,1024]{1,0:T(8,128)(2,1)}) %all-gather.5.cloned.1.call-update) | async-done | bytes 2097168 | tf_op jit(solution)/shard_map/all_gather | solution.py:24
  40.4 0.0 copy-start
  40.4 287.8 %all-gather.3.cloned.1.call-done = bf16[8192,1024]{1,0:T(8,128)(2,1)} async-done(((bf16[8192,256]{1,0:T(8,128)(2,1)}), bf16[8192,1024]{1,0:T(8,128)(2,1)}) %all-gather.3.cloned.1.call-update) | async-done | bytes 16777232 | tf_op jit(solution)/shard_map/all_gather | solution.py:25
  328.2 34.3 %multiply_convert_fusion = (bf16[8192,1024]{1,0:T(8,128)(2,1)}, f32[8192,1024]{1,0:T(8,128)}) fusion(bf16[8192,1024]{1,0:T(8,128)(2,1)} %all-gather.3.cloned.1.call-done, bf16[1024,1024]{1,0:T(8,128)(2,1)} %all-gather.5.cloned.1.call-done), kind=kOutput, calls=%fused_computation.9 | convolution fusion | flops 17255366656 | bytes 69206016 | tf_op jit(solution)/shard_map/dot_general | solution.py:26
  362.6 0.0 copy-done
  362.6 40.1 %convert_bitcast_fusion = bf16[1024,8192]{0,1:T(8,128)(2,1)} fusion(bf16[1024,1024]{1,0:T(8,128)(2,1)S(1)} %copy-done, f32[8192,1024]{1,0:T(8,128)} %get-tuple-element.3, bf16[8192,1024]{1,0:T(8,128)(2,1)} %param.5), kind=kOutput, calls=%fused_computation.10 | convolution fusion | flops 17356029952 | bytes 69206016 | tf_op jit(solution)/shard_map/dot_general | solution.py:30
  402.7 0.0 reduce-scatter.2.cloned.1.call-update
  402.7 278.8 %reduce-scatter.2.cloned.1.call-done = bf16[256,8192]{0,1:T(8,128)(2,1)} async-done(((bf16[1024,8192]{0,1:T(8,128)(2,1)}), bf16[256,8192]{0,1:T(8,128)(2,1)}) %reduce-scatter.2.cloned.1.call-update) | async-done | bytes 4194320 | tf_op jit(solution)/shard_map/reduce_scatter | solution.py:29
Async XLA Ops:
  7.2 33.2 %all-gather.5.cloned.1.call-start = ((), (), s32[]{:S(2)}) async-start(), calls=%async_computation.2 | async-start | bytes 2359296 | tf_op jit(solution)/shard_map/all_gather | solution.py:24
  7.9 320.3 %all-gather.3.cloned.1.call-start = ((), (), s32[]{:S(2)}) async-start(), calls=%async_computation.1 | async-start | bytes 20971520 | tf_op jit(solution)/shard_map/all_gather | solution.py:25
  8.6 672.9 %reduce-scatter.2.cloned.1.call-start = ((), (), s32[]{:S(2)}) async-start(), calls=%async_computation.3 | async-start | bytes 20971520 | tf_op jit(solution)/shard_map/reduce_scatter | solution.py:29
  40.4 322.2 %copy-start = (bf16[1024,1024]{1,0:T(8,128)(2,1)S(1)}, bf16[1024,1024]{1,0:T(8,128)(2,1)}, u32[]{:S(2)}) copy-start(bf16[1024,1024]{1,0:T(8,128)(2,1)} %all-gather.5.cloned.1.call-done) | copy-start | bytes 6291460
Sparse Core Ops, SparseCore 0:
  9.9 30.4 all-gather.4
  41.9 286.2 all-gather.2
  402.9 278.6 reduce-scatter.1
where the time goes:
time: 688 us
  waiting for transfers between devices  600 us (87%)
  matrix products  74.5 us (11%)
  between operations  13.7 us (2%)
    all_gather x1, waiting for transfers between devices, per_device(): token_rows = lax.all_gather(tokens, 'col', axis=1, tiled=True)  288 us
    reduce_scatter x1, waiting for transfers between devices, per_device(): lax.psum_scatter(lax.dot_general(column_panel, pre_grad, (((1,), (1,)), (...  279 us
    dot_general x1, matrix products, per_device(): lax.dot_general(column_panel, pre_grad, (((1,), (1,)), ((), ())), preferr...  40.1 us
    dot_general x1, matrix products, per_device(): jnp.dot(token_rows, column_panel, preferred_element_type=jnp.float32)  34.3 us
    all_gather x1, waiting for transfers between devices, per_device(): column_panel = lax.all_gather(up_weight, 'row', axis=0, tiled=True)  31.7 us
  transfers between devices with their start and end apart: 3, of which 3 were waited for; matrix products, arithmetic and copies ran while one was open for 0% of the time, Pallas kernels for 0%

commit v1 on v0

--- a/solution.py
+++ b/solution.py
@@ -22,7 +22,20 @@
 
 def per_device(tokens, up_weight, hidden_grad):
     column_panel = lax.all_gather(up_weight, "row", axis=0, tiled=True)
-    token_rows = lax.all_gather(tokens, "col", axis=1, tiled=True)
+    devs = lax.axis_size("col")
+    all_rows = [(s, (s + 1) % devs) for s in range(devs)]
+    far_arr, y1 = ([tokens], [tokens])
+    views = [(s, (s - 1) % devs) for s in range(devs)]
+    for _ in range(devs // 2):
+        far_arr.append(lax.ppermute(far_arr[-1], axis_name="col", perm=all_rows))
+    for _ in range((devs - 1) // 2):
+        x_new = lax.ppermute(y1[-1], axis_name="col", perm=views)
+        y1.append(x_new)
+    token_rows = jnp.roll(
+        jnp.concatenate([*far_arr[::-1], *y1[1:]], axis=1),
+        shift=(lax.axis_index("col") - devs // 2) * tokens.shape[1],
+        axis=1,
+    )
     preact = jnp.dot(token_rows, column_panel, preferred_element_type=jnp.float32)
     hidden = gelu_value(preact).astype(jnp.bfloat16)
     pre_grad = (hidden_grad.astype(jnp.float32) * gelu_slope(preact)).astype(jnp.bfloat16)

time: 688 us -> 668 us (0.971)
  waiting for transfers between devices: 600 us -> 538 us
  local copies, waits for them, and re-layouts: 0.01 us -> 33.9 us
  starting transfers between devices: 0.11 us -> 7.01 us
    all_gather x1 -> x0, waiting for transfers between devices: 288 us -> none  [per_device(): token_rows = lax.all_gather(tokens, 'col', axis=1, tiled=True)]
    ppermute x0 -> x3, waiting for transfers between devices: none -> 257 us  [the longest x2 185 us: per_device(): far_arr.append(lax.ppermute(far_arr[-1], axis_name='col', perm=all_rows))]
    all_gather x1, waiting for transfers between devices: 31.7 us -> 0.01 us  [per_device(): column_panel = lax.all_gather(up_weight, 'row', axis=0, tiled=True)]
    unnamed x2 -> x11, local copies, waits for them, and re-layouts: 0.01 us -> 29.4 us
    ppermute x0 -> x3, starting transfers between devices: none -> 6.93 us  [the longest x1 3.82 us: per_device(): x_new = lax.ppermute(y1[-1], axis_name='col', perm=views)]
  transfers between devices with their start and end apart: 3 -> 5, of which waited for: 3 -> 4; matrix products, arithmetic and copies ran while one was open for 0% -> 5% of each run, Pallas kernels for 0% -> 0%
where the time goes in v1:
time: 668 us; the launch traced here: 667 us
  waiting for transfers between devices  538 us (81%)
  matrix products  74.7 us (11%)
  local copies, waits for them, and re-layouts  33.9 us (5%)
  between operations  14.1 us (2%)
  starting transfers between devices  7.01 us (1%)
    reduce_scatter x1, waiting for transfers between devices, per_device(): lax.psum_scatter(lax.dot_general(column_panel, pre_grad, (((1,), (1,)), (...  280 us
    ppermute x2, waiting for transfers between devices, per_device(): far_arr.append(lax.ppermute(far_arr[-1], axis_name='col', perm=all_rows))  185 us
    ppermute x1, waiting for transfers between devices, per_device(): x_new = lax.ppermute(y1[-1], axis_name='col', perm=views)  72.9 us
    dot_general x1, matrix products, per_device(): lax.dot_general(column_panel, pre_grad, (((1,), (1,)), ((), ())), preferr...  40.1 us
    dot_general x1, matrix products, per_device(): jnp.dot(token_rows, column_panel, preferred_element_type=jnp.float32)  34.5 us
    unnamed x11, local copies, waits for them, and re-layouts  29.4 us
  transfers between devices with their start and end apart: 5, of which 4 were waited for; matrix products, arithmetic and copies ran while one was open for 5% of the time, Pallas kernels for 0%

profile of v1, /device:TPU:0, one launch (start us, length us, event | category | flops | bytes accessed | tf_op | source)
XLA Modules:
  0.0 667.5 jit_solution(7844224912224045310)
XLA Ops:
  7.2 0.0 all-gather.2.cloned.1.call-start
  7.2 3.1 collective-permute-start
  10.3 92.9 %collective-permute-done = bf16[8192,256]{1,0:T(8,128)(2,1)} collective-permute-done((bf16[8192,256]{1,0:T(8,128)(2,1)}, bf16[8192,256]{1,0:T(8,128)(2,1)}, u32[]{:S(2)}, u32[]{:S(2)}) %collective-permute-start) | collective-permute-done | bytes 4194336 | tf_op jit(solution)/shard_map/ppermute | solution.py:30
  103.2 0.0 collective-permute-start.1
  103.2 3.8 collective-permute-start.2
  107.1 0.0 all-gather.2.cloned.1.call-update
  107.1 0.0 reduce-scatter.2.cloned.1.call-start
  107.2 0.0 copy-start
  107.2 91.6 %collective-permute-done.1 = bf16[8192,256]{1,0:T(8,128)(2,1)} collective-permute-done((bf16[8192,256]{1,0:T(8,128)(2,1)}, bf16[8192,256]{1,0:T(8,128)(2,1)}, u32[]{:S(2)}, u32[]{:S(2)}) %collective-permute-start.1) | collective-permute-done | bytes 4194336 | tf_op jit(solution)/shard_map/ppermute | solution.py:30
  198.8 4.5 constant_dynamic-update-slice_fusion.7
  203.3 4.5 constant_dynamic-update-slice_fusion.6
  207.8 4.5 constant_dynamic-update-slice_fusion.5
  212.3 72.9 %collective-permute-done.2 = bf16[8192,256]{1,0:T(8,128)(2,1)} collective-permute-done((bf16[8192,256]{1,0:T(8,128)(2,1)}, bf16[8192,256]{1,0:T(8,128)(2,1)}, u32[]{:S(2)}, u32[]{:S(2)}) %collective-permute-start.2) | collective-permute-done | bytes 4194336 | tf_op jit(solution)/shard_map/ppermute | solution.py:32
  285.2 4.5 constant_dynamic-update-slice_fusion.4
  289.7 4.5 constant_dynamic-update-slice_fusion.3
  294.2 4.5 constant_dynamic-update-slice_fusion.2
  298.7 0.0 copy-done
  298.7 2.4 constant_dynamic-update-slice_fusion.1
  301.1 4.5 constant_dynamic-update-slice_fusion
  305.6 0.0 all-gather.2.cloned.1.call-done
  305.6 0.0 copy-start.1
  305.6 34.5 %multiply_convert_fusion = (bf16[8192,1024]{1,0:T(8,128)(2,1)}, f32[8192,1024]{1,0:T(8,128)}) fusion(bf16[1024,1024]{1,0:T(8,128)(2,1)} %all-gather.2.cloned.1.call-done, bf16[8192,2048]{1,0:T(8,128)(2,1)} %constant_dynamic-update-slice_fusion, s32[]{:T(128)S(6)} %select_n.14), kind=kOutput, calls=%fused_computation.9 | convolution fusion | flops 17255366656 | bytes 69206016 | tf_op jit(solution)/shard_map/dot_general | solution.py:39
  340.1 0.0 copy-done.1
  340.1 40.1 %convert_bitcast_fusion = bf16[1024,8192]{0,1:T(8,128)(2,1)} fusion(bf16[1024,1024]{1,0:T(8,128)(2,1)S(1)} %copy-done.1, f32[8192,1024]{1,0:T(8,128)} %get-tuple-element.3, bf16[8192,1024]{1,0:T(8,128)(2,1)} %param.5), kind=kOutput, calls=%fused_computation.10 | convolution fusion | flops 17356029952 | bytes 69206016 | tf_op jit(solution)/shard_map/dot_general | solution.py:43
  380.2 0.0 reduce-scatter.2.cloned.1.call-update
  380.3 280.4 %reduce-scatter.2.cloned.1.call-done = bf16[256,8192]{0,1:T(8,128)(2,1)} async-done(((bf16[1024,8192]{0,1:T(8,128)(2,1)}), bf16[256,8192]{0,1:T(8,128)(2,1)}) %reduce-scatter.2.cloned.1.call-update) | async-done | bytes 4194320 | tf_op jit(solution)/shard_map/reduce_scatter | solution.py:42
Async XLA Ops:
  7.2 298.4 %all-gather.2.cloned.1.call-start = ((), (), s32[]{:S(2)}) async-start(), calls=%async_computation.1 | async-start | bytes 2359296 | tf_op jit(solution)/shard_map/all_gather | solution.py:24
  7.2 96.0 %collective-permute-start = (bf16[8192,256]{1,0:T(8,128)(2,1)}, bf16[8192,256]{1,0:T(8,128)(2,1)}, u32[]{:S(2)}, u32[]{:S(2)}) collective-permute-start(bf16[8192,256]{1,0:T(8,128)(2,1)} %param.3), channel_id=1, source_target_pairs={{0,1},{1,2},{2,3},{3,0},{4,5},{5,6},{6,7},{7,4},{8,9},{9,10},{10,1... | collective-permute-start | bytes 12582920 | tf_op jit(solution)/shard_map/ppermute | solution.py:30
  103.2 95.6 %collective-permute-start.1 = (bf16[8192,256]{1,0:T(8,128)(2,1)}, bf16[8192,256]{1,0:T(8,128)(2,1)}, u32[]{:S(2)}, u32[]{:S(2)}) collective-permute-start(bf16[8192,256]{1,0:T(8,128)(2,1)} %collective-permute-done), channel_id=1, source_target_pairs={{0,1},{1,2},{2,3},{3,0},{4,5},{5,6},{6,7},{7,4},{8,9},{9,10},{10,1... | collective-permute-start | bytes 12582920 | tf_op jit(solution)/shard_map/ppermute | solution.py:30
  103.2 181.9 %collective-permute-start.2 = (bf16[8192,256]{1,0:T(8,128)(2,1)}, bf16[8192,256]{1,0:T(8,128)(2,1)}, u32[]{:S(2)}, u32[]{:S(2)}) collective-permute-start(bf16[8192,256]{1,0:T(8,128)(2,1)} %param.3), channel_id=1, source_target_pairs={{0,3},{1,0},{2,1},{3,2},{4,7},{5,4},{6,5},{7,6},{8,11},{9,8},{10,9... | collective-permute-start | bytes 12582920 | tf_op jit(solution)/shard_map/ppermute | solution.py:32
  107.1 553.6 %reduce-scatter.2.cloned.1.call-start = ((), (), s32[]{:S(2)}) async-start(), calls=%async_computation.2 | async-start | bytes 20971520 | tf_op jit(solution)/shard_map/reduce_scatter | solution.py:42
  107.2 191.6 %copy-start = (bf16[8192,256]{1,0:T(8,128)(2,1)S(1)}, bf16[8192,256]{1,0:T(8,128)(2,1)}, u32[]{:S(2)}) copy-start(bf16[8192,256]{1,0:T(8,128)(2,1)} %param.3) | copy-start | bytes 12582916
  305.6 34.5 %copy-start.1 = (bf16[1024,1024]{1,0:T(8,128)(2,1)S(1)}, bf16[1024,1024]{1,0:T(8,128)(2,1)}, u32[]{:S(2)}) copy-start(bf16[1024,1024]{1,0:T(8,128)(2,1)} %all-gather.2.cloned.1.call-done) | copy-start | bytes 6291460
Sparse Core Ops, SparseCore 0:
  107.2 25.9 all-gather.1
  380.4 280.2 reduce-scatter.1
